TPU v7x, 32 devices: a whole 2x2x4 slice. The times are simulated.
32 devices in a mesh: groups: 2 (over x), hit: 8 (over z, y), query: 2 (over core).
Axes of the slice: x: 2, y: 2, z: 4, core: 2. Of those that a mesh axis runs over, the one named last changes fastest.
Arguments:
- hits: bfloat16 [16384, 512], P(('groups', 'hit', 'query')), parts along dimension 0, may hold values from -24 to 24
- order: int32 [32, 512], P(('groups', 'hit', 'query')), parts along dimension 0, may hold values from 0 to 511, each once within a row
- valid: int32 [16384], P(('groups', 'hit', 'query')), parts along dimension 0, may hold values 0 or 1
- reach: int32 [16384], P(('groups', 'hit', 'query')), parts along dimension 0, may hold values from 128 to 512, as said below
- enc_wq: bfloat16 [512, 512], replicated, may hold values from -3 to 3
- enc_wk: bfloat16 [512, 512], replicated, may hold values from -1 to 1
- enc_wv: bfloat16 [512, 512], replicated, may hold values from -0.25 to 0.25
- enc_wo: bfloat16 [512, 512], replicated, may hold values from -0.25 to 0.25
- enc_gain1: float32 [512], replicated, may hold values from 0.5 to 1.5
- ffn_up: bfloat16 [512, 2048], replicated, may hold values from -0.25 to 0.25
- ffn_down: bfloat16 [2048, 512], replicated, may hold values from -0.125 to 0.125
- enc_gain2: float32 [512], replicated, may hold values from 0.5 to 1.5
- object_queries: bfloat16 [512, 512], P(('groups', 'hit', 'query')), parts along dimension 0, may hold values from -48 to 48
- dec_wq: bfloat16 [512, 512], replicated, may hold values from -8 to 8
- dec_wk: bfloat16 [512, 512], replicated, may hold values from -0.25 to 0.25
- dec_wv: bfloat16 [512, 512], replicated, may hold values from -0.25 to 0.25
- dec_wo: bfloat16 [512, 512], replicated, may hold values from -0.25 to 0.25
- dec_gain: float32 [512], replicated, may hold values from 0.5 to 1.5
- out_proj: bfloat16 [512, 512], replicated, may hold values from -0.25 to 0.25
Outputs:
- encoded: bfloat16 [16384, 512], P(('groups', 'hit', 'query')), parts along dimension 0
- decoded: bfloat16 [512, 512], P(('groups', 'hit', 'query')), parts along dimension 0
There are 2 independent parts, one for each index of `groups`. A program takes and returns all parts, laid end to end along the dimension named above; an argument that names none is the same for every part. Nothing has to cross between parts.
Inputs may be any that keep to these rules, and one draw needn't show every extreme that they name: The first hit of every block of 512 arrival positions has reach 512.
All inputs are finite; a program needn't handle non-finite values. No bound on the sum of `valid` on one device may be relied on, other than what follows from the above.
Results may differ from a plain program's by a relative error of at most 0.035.
Values may be sent and summed in bfloat16 or wider, within the bound.
No kernel may reach another device: no remote copies, remote signals or barrier semaphores. Data moves between devices by JAX's collectives and lax.ppermute only.
A program may use at most 192 MiB of HBM per device.

v0:
```python
import math

import jax
import jax.numpy as jnp
from jax import lax
from jax.sharding import PartitionSpec as P

D = 512
HEADS = 8
WINDOW = 512


def padded(cells, sides, width):
    for axis, dim in sides:
        count = lax.axis_size(axis)
        head = lax.slice_in_dim(cells, 0, width, axis=dim)
        tail = lax.slice_in_dim(cells, cells.shape[dim] - width, cells.shape[dim], axis=dim)
        cells = jnp.concatenate(
            [
                lax.ppermute(tail, axis, [(i, (i + 1) % count) for i in range(count)]),
                cells,
                lax.ppermute(head, axis, [((i + 1) % count, i) for i in range(count)]),
            ],
            axis=dim,
        )
    return cells


def joined(value, axis, combine):
    everything = jax.tree.map(lambda part: lax.all_gather(part, axis), value)
    leading = jax.tree.map(lambda part: part[0], everything)

    def lap(k, so_far):
        return combine(so_far, jax.tree.map(lambda part: part[k], everything))

    return lax.fori_loop(1, lax.axis_size(axis), lap, leading)


def project(rows, weight):
    return jnp.dot(rows, weight, preferred_element_type=jnp.float32).astype(jnp.bfloat16)


def rms_norm(values, gain):
    scale = lax.rsqrt(jnp.mean(values * values, axis=-1, keepdims=True) + 1e-05)
    return values * scale * gain


def band_attention(queries, keys, values, key_valid, reach):
    count = queries.shape[0]
    span = keys.shape[0]
    margin = (span - count) // 2
    width = queries.shape[1] // HEADS
    query_heads = queries.reshape(count, HEADS, width)
    key_heads = keys.reshape(span, HEADS, width)
    value_heads = values.reshape(span, HEADS, width)
    scores = jnp.einsum(
        "qhd,khd->hqk", query_heads, key_heads, preferred_element_type=jnp.float32
    ) * (1.0 / math.sqrt(width))
    offset = jnp.arange(span, dtype=jnp.int32)[None, :] - (
        jnp.arange(count, dtype=jnp.int32)[:, None] + margin
    )
    allowed = (jnp.abs(offset) <= reach[:, None]) & ((key_valid[None, :] > 0) | (offset == 0))
    scores = jnp.where(allowed[None], scores, -jnp.inf)
    peak = jnp.max(scores, axis=2, keepdims=True)
    expo = jnp.where(allowed[None], jnp.exp(scores - peak), 0.0)
    probs = (expo / jnp.sum(expo, axis=2, keepdims=True)).astype(jnp.bfloat16)
    context = jnp.einsum("hqk,khd->qhd", probs, value_heads, preferred_element_type=jnp.float32)
    return context.reshape(count, HEADS * width).astype(jnp.bfloat16)


def encoder_tail(context, sorted_hits, enc_wo, enc_gain1, ffn_up, ffn_down, enc_gain2):
    attn_res = jnp.dot(context, enc_wo, preferred_element_type=jnp.float32) + sorted_hits.astype(
        jnp.float32
    )
    middle = rms_norm(attn_res, enc_gain1).astype(jnp.bfloat16)
    hidden = jax.nn.gelu(
        jnp.dot(middle, ffn_up, preferred_element_type=jnp.float32), approximate=True
    ).astype(jnp.bfloat16)
    ffn_res = jnp.dot(hidden, ffn_down, preferred_element_type=jnp.float32) + middle.astype(
        jnp.float32
    )
    return rms_norm(ffn_res, enc_gain2).astype(jnp.bfloat16)


def span_partial(queries, keys, values):
    count = queries.shape[0]
    span = keys.shape[0]
    width = queries.shape[1] // HEADS
    query_heads = queries.reshape(count, HEADS, width)
    key_heads = keys.reshape(span, HEADS, width)
    value_heads = values.reshape(span, HEADS, width)
    scores = jnp.einsum(
        "qhd,khd->qhk", query_heads, key_heads, preferred_element_type=jnp.float32
    ) * (1.0 / math.sqrt(width))
    peak = jnp.max(scores, axis=2)
    expo = jnp.exp(scores - peak[:, :, None])
    total = jnp.sum(expo, axis=2)
    weights = expo.astype(jnp.bfloat16)
    output = jnp.einsum("qhk,khd->qhd", weights, value_heads, preferred_element_type=jnp.float32)
    return (peak, total, output.reshape(count, HEADS * width))


def merge_partials(first, second):
    width = D // HEADS
    peak = jnp.maximum(first[0], second[0])
    left = jnp.exp(first[0] - peak)
    right = jnp.exp(second[0] - peak)
    total = first[1] * left + second[1] * right
    output = first[2] * jnp.repeat(left, width, axis=1) + second[2] * jnp.repeat(
        right, width, axis=1
    )
    return (peak, total, output)


def on_device(
    hits,
    order,
    valid,
    reach,
    enc_wq,
    enc_wk,
    enc_wv,
    enc_wo,
    enc_gain1,
    ffn_up,
    ffn_down,
    enc_gain2,
    object_queries,
    dec_wq,
    dec_wk,
    dec_wv,
    dec_wo,
    dec_gain,
    out_proj,
):
    rows = hits.shape[0]
    place = order[0]
    sorted_hits = hits[place]
    sorted_valid = valid[place].astype(jnp.bfloat16)
    sorted_reach = reach[place]
    queries = project(sorted_hits, enc_wq)
    wide_hits, wide_valid = (
        padded(sorted_hits, ((("hit", "query"), 0),), WINDOW),
        padded(sorted_valid, ((("hit", "query"), 0),), WINDOW),
    )
    wide_keys = project(wide_hits, enc_wk)
    wide_values = project(wide_hits, enc_wv)
    block = 512

    def attend(index):
        start = index * block
        return band_attention(queries, wide_keys, wide_values, wide_valid, sorted_reach)

    context = lax.map(attend, jnp.arange(rows // block, dtype=jnp.int32)).reshape(
        rows, queries.shape[1]
    )
    encoded = encoder_tail(context, sorted_hits, enc_wo, enc_gain1, ffn_up, ffn_down, enc_gain2)
    local_queries = project(object_queries, dec_wq)
    span_keys, span_values = (
        lax.all_gather(project(encoded, dec_wk), "query", axis=0, tiled=True),
        lax.all_gather(project(encoded, dec_wv), "query", axis=0, tiled=True),
    )
    all_queries = lax.all_gather(local_queries, "hit", axis=0, tiled=True)
    count = all_queries.shape[0]
    qblock = 512 if count % 512 == 0 else count

    def partial_block(index):
        return span_partial(all_queries, span_keys, span_values)

    peaks, totals, outputs = lax.map(partial_block, jnp.arange(count // qblock, dtype=jnp.int32))
    width = D // HEADS
    peaks = peaks.reshape(count, HEADS)
    totals = totals.reshape(count, HEADS)
    outputs = outputs.reshape(count, HEADS * width)
    owned = object_queries.shape[0]
    highest, merged_total, merged_out = joined((peaks, totals, outputs), "hit", merge_partials)
    start = lax.axis_index("hit") * owned
    numer = lax.dynamic_slice_in_dim(merged_out, start, owned, 0)
    denom = lax.dynamic_slice_in_dim(merged_total, start, owned, 0)
    cross = (numer / jnp.repeat(denom, width, axis=1)).astype(jnp.bfloat16)
    dec_res = jnp.dot(cross, dec_wo, preferred_element_type=jnp.float32) + object_queries.astype(
        jnp.float32
    )
    normed = rms_norm(dec_res, dec_gain).astype(jnp.bfloat16)
    decoded = jnp.dot(normed, out_proj, preferred_element_type=jnp.float32).astype(jnp.bfloat16)
    return (encoded, decoded)


def solution(mesh):
    in_specs = (
        P(("groups", "hit", "query"), None),
        P(("groups", "hit", "query"), None),
        P(("groups", "hit", "query")),
        P(("groups", "hit", "query")),
        P(),
        P(),
        P(),
        P(),
        P(),
        P(),
        P(),
        P(),
        P(("groups", "hit", "query"), None),
        P(),
        P(),
        P(),
        P(),
        P(),
        P(),
    )
    out_specs = (P(("groups", "hit", "query"), None), P(("groups", "hit", "query"), None))
    return jax.shard_map(
        on_device, mesh=mesh, in_specs=in_specs, out_specs=out_specs, check_vma=False
    )
```

profile of v0, /device:TPU:0, one launch (start us, length us, event | category | flops | bytes accessed | tf_op | source)
XLA Modules:
  0.0 208.7 jit_solution(11262240188574677869)
XLA Ops:
  7.2 0.8 compare_select_fusion
  8.1 3.1 %gather_fusion = bf16[512,512]{1,0:T(8,128)(2,1)S(1)} fusion(bf16[512,512]{1,0:T(8,128)(2,1)} %param.21, s32[1024]{0:T(1024)S(1)} %pad_clamp_fusion), kind=kCustom, calls=%fused_computation | custom fusion | bytes 1050624 | tf_op jit(solution)/shard_map/gather | solution.py:138
  11.2 0.5 collective-permute-start
  11.7 5.0 %collective-permute-start.1 = (bf16[512,512]{1,0:T(8,128)(2,1)S(1)}, bf16[512,512]{1,0:T(8,128)(2,1)}, u32[]{:S(2)}, u32[]{:S(2)}) collective-permute-start(bf16[512,512]{1,0:T(8,128)(2,1)S(1)} %gather_fusion), channel_id=1, source_target_pairs={{1,0},{2,1},{3,2},{4,3},{5,4},{6,5},{7,6},{8,7},{9,8},{10,9},{11,1... | collective-permute-start | bytes 1572872 | tf_op jit(solution)/shard_map/ppermute | solution.py:22
  16.8 3.5 %gather_fusion.2 = s32[512]{0:T(512)S(1)} fusion(s32[512]{0:T(512)S(1)} %copy-done.1, s32[1024]{0:T(1024)S(1)} %pad_clamp_fusion), kind=kCustom, calls=%fused_computation.2 | custom fusion | bytes 6144 | tf_op jit(solution)/shard_map/gather | solution.py:139
  20.4 4.4 %collective-permute-start.3 = (bf16[512]{0:T(512)(128)(2,1)S(1)}, bf16[512]{0:T(512)(128)(2,1)S(1)}, u32[]{:S(2)}, u32[]{:S(2)}) collective-permute-start(bf16[512]{0:T(512)(128)(2,1)S(1)} %convert_element_type.70), channel_id=1, source_target_pairs={{1,0},{2,1},{3,2},{4,3},{5,4},{6,5},{7,6},{8,7},{9,8},{10,9},{11,1... | collective-permute-start | bytes 3080 | tf_op jit(solution)/shard_map/ppermute | solution.py:22
  24.8 2.3 %convolution_convert_fusion.4 = bf16[512,512]{0,1:T(8,128)(2,1)} fusion(bf16[512,512]{1,0:T(8,128)(2,1)S(1)} %gather_fusion, bf16[512,512]{1,0:T(8,128)(2,1)} %param.25), kind=kOutput, calls=%fused_computation.52 | convolution fusion | flops 268697600 | bytes 1572864 | tf_op jit(solution)/shard_map/dot_general | solution.py:40
  27.1 0.2 copy.37
  27.3 3.5 %gather_fusion.1 = s32[512]{0:T(512)S(1)} fusion(s32[512]{0:T(512)S(1)} %copy-done.2, s32[1024]{0:T(1024)S(1)} %pad_clamp_fusion), kind=kCustom, calls=%fused_computation.1 | custom fusion | bytes 6144 | tf_op jit(solution)/shard_map/gather | solution.py:140
  30.9 2.5 %fusion.21 = pred[512,1536]{1,0:T(8,128)(4,1)} fusion(s32[512]{0:T(512)S(1)} %gather_fusion.1, s32[512]{0:T(512)S(1)} %iota_add_fusion, pred[1536]{0:T(1024)(128)(4,1)S(1)} %maximum_compare_fusion), kind=kLoop, calls=%fused_computation.39 | loop fusion | flops 4718592 | bytes 792064 | tf_op jit(solution)/shard_map/while/body/eval_jaxpr/and | solution.py:62
  33.4 1.1 constant_dynamic-update-slice_fusion.2
  34.5 1.1 constant_dynamic-update-slice_fusion
  35.6 3.3 %convolution_convert_fusion = bf16[1536,512]{0,1:T(8,128)(2,1)} fusion(bf16[1536,512]{1,0:T(8,128)(2,1)S(1)} %constant_dynamic-update-slice_fusion, bf16[512,512]{1,0:T(8,128)(2,1)} %param.26), kind=kOutput, calls=%fused_computation.41 | convolution fusion | flops 806092800 | bytes 3670016 | tf_op jit(solution)/shard_map/dot_general | solution.py:40
  38.9 2.2 %convolution_convert_fusion.1 = bf16[1536,512]{0,1:T(8,128)(2,1)} fusion(bf16[1536,512]{1,0:T(8,128)(2,1)S(1)} %constant_dynamic-update-slice_fusion, bf16[512,512]{1,0:T(8,128)(2,1)S(1)} %copy-done.11), kind=kOutput, calls=%fused_computation.42 | convolution fusion | flops 806092800 | bytes 3670016 | tf_op jit(solution)/shard_map/dot_general | solution.py:40
  41.1 16.0 %fusion.47 = (f32[8,512]{1,0:T(8,128)S(1)}, f32[8,512,1536]{2,1,0:T(8,128)}) fusion(pred[512,1536]{1,0:T(8,128)(4,1)S(1)} %copy-done.4, bf16[512,8,64]{0,2,1:T(8,128)(2,1)} %bitcast.90, bf16[1536,8,64]{0,2,1:T(8,128)(2,1)} %bitcast.97), kind=kOutput, calls=%fused_computation.87 | convolution fusion | flops 836765184 | bytes 28065792 | tf_op jit(solution)/shard_map/while/body/eval_jaxpr/sub | solution.py:65
  57.1 11.0 %fusion.32 = bf16[8,64,512]{2,1,0:T(8,128)(2,1)S(1)} fusion(bf16[1536,8,64]{0,2,1:T(8,128)(2,1)} %bitcast.96, f32[8,512,1536]{2,1,0:T(8,128)} %get-tuple-element.255, f32[8,512]{1,0:T(8,128)S(1)} %get-tuple-element.254), kind=kOutput, calls=%fused_computation.49 | convolution fusion | flops 818151424 | bytes 27279360 | tf_op jit(solution)/shard_map/while/body/eval_jaxpr/hqk,khd->qhd/dot_general | solution.py:67
  68.1 1.5 multiply_reduce_fusion.1
  69.6 6.4 %multiply_reduce_fusion = (f32[512]{0:T(512)S(1)}, f32[512,512]{0,1:T(8,128)}) fusion(f32[512]{0:T(512)S(1)} %copy-done.12, f32[512,512]{0,1:T(8,128)} %get-tuple-element.257, f32[512]{0:T(512)S(1)} %add_rsqrt_fusion.1, bf16[2048,512]{1,0:T(8,128)(2,1)S(1)} %copy-done, bf16[512,2048]{1,0:T(8,128)(2,1)} %param.30), kind=kOutput, calls=%fused_computation.57 | convolution fusion | flops 2159541760 | bytes 6297600 | tf_op jit(solution)/shard_map/dot_general | solution.py:79
  76.0 1.4 multiply_convert_fusion
  77.4 2.5 %convolution_convert_fusion.3 = bf16[512,512]{1,0:T(8,128)(2,1)} fusion(bf16[512,512]{0,1:T(8,128)(2,1)S(1)} %multiply_convert_fusion, bf16[512,512]{1,0:T(8,128)(2,1)} %param.35), kind=kOutput, calls=%fused_computation.51 | convolution fusion | flops 268697600 | bytes 1572864 | tf_op jit(solution)/shard_map/dot_general | solution.py:40
  80.0 2.4 %convolution_convert_fusion.2 = bf16[512,512]{1,0:T(8,128)(2,1)} fusion(bf16[512,512]{0,1:T(8,128)(2,1)S(1)} %multiply_convert_fusion, bf16[512,512]{1,0:T(8,128)(2,1)} %param.36), kind=kOutput, calls=%fused_computation.50 | convolution fusion | flops 268697600 | bytes 1572864 | tf_op jit(solution)/shard_map/dot_general | solution.py:40
  82.5 0.2 convolution_convert_fusion.6
  82.6 30.5 %all_gather.19 = bf16[128,512]{1,0:T(8,128)(2,1)S(1)} all-gather(bf16[16,512]{1,0:T(8,128)(2,1)S(1)} %convolution_convert_fusion.6), channel_id=1, replica_groups=mesh['groups'=2,'hit'=8,'query'=2] {'hit'}, dimensions={0}, use_global_device_ids=true | all-gather | bytes 147456 | tf_op jit(solution)/shard_map/all_gather | solution.py:163
  113.3 1.5 copy.38
  114.8 2.8 %bitcast_reduce_fusion = (f32[128,8]{0,1:T(8,128)S(1)}, f32[8,1024,128]{2,1,0:T(8,128)}) fusion(bf16[1024,8,64]{0,2,1:T(8,128)(2,1)S(1)} %bitcast.87, bf16[128,8,64]{0,2,1:T(8,128)(2,1)S(1)} %bitcast.91), kind=kOutput, calls=%fused_computation.32 | convolution fusion | flops 136313856 | bytes 5378048 | tf_op jit(solution)/shard_map/while/body/eval_jaxpr/qhd,khd->qhk/dot_general | solution.py:92
  117.6 1.5 copy.40
  119.1 3.0 %fusion.23 = f32[8,64,128]{2,1,0:T(8,128)S(1)} fusion(bf16[1024,8,64]{0,2,1:T(8,128)(2,1)S(1)} %bitcast.88, f32[8,1024,128]{2,1,0:T(8,128)} %get-tuple-element.261, f32[128,8]{0,1:T(8,128)S(1)} %get-tuple-element.260), kind=kOutput, calls=%fused_computation.43 | convolution fusion | flops 137363456 | bytes 5509120 | tf_op jit(solution)/shard_map/while/body/eval_jaxpr/qhk,khd->qhd/dot_general | solution.py:99
  122.1 0.8 copy.42
  123.0 2.0 copy.45
  125.1 2.9 %fusion.19 = f32[128,8]{0,1:T(8,128)S(1)} fusion(f32[8,1024,128]{2,1,0:T(8,128)} %get-tuple-element.261, f32[128,8]{0,1:T(8,128)S(1)} %get-tuple-element.260), kind=kLoop, calls=%fused_computation.35 | loop fusion | flops 3144704 | bytes 4202496 | tf_op jit(solution)/shard_map/while/body/eval_jaxpr/reduce_sum | solution.py:97
  127.9 31.0 %all-gather.1 = f32[1024,8]{0,1:T(8,128)S(1)} all-gather(f32[128,8]{0,1:T(8,128)S(1)} %fusion.19), channel_id=3, replica_groups=mesh['groups'=2,'hit'=8,'query'=2] {'hit'}, dimensions={0}, use_global_device_ids=true | all-gather | bytes 36864 | tf_op jit(solution)/shard_map/all_gather | solution.py:30
  159.0 30.8 %all-gather = f32[1024,8]{0,1:T(8,128)S(1)} all-gather(f32[128,8]{0,1:T(8,128)S(1)} %get-tuple-element.260), channel_id=2, replica_groups=mesh['groups'=2,'hit'=8,'query'=2] {'hit'}, dimensions={0}, use_global_device_ids=true | all-gather | bytes 36864 | tf_op jit(solution)/shard_map/all_gather | solution.py:30
  189.7 1.0 slice_bitcast_fusion
  190.7 0.1 copy.43
  190.9 8.8 %while.12 = (s32[]{:T(128)}, f32[128,8]{0,1:T(8,128)S(1)}, f32[128,8]{0,1:T(8,128)S(1)}, f32[128,512]{0,1:T(8,128)S(1)}, f32[8,128,8]{1,2,0:T(8,128)S(1)}, /*ind...) while((s32[]{:T(128)}, f32[128,8]{0,1:T(8,128)S(1)}, ...), condition=%wide.region_7.8_spmd, body=%wide.region_6.7_spmd.sunk | while | flops 202757 | bytes 1876119 | solution.py:36
  190.9 1.0 constant_dynamic-slice_fusion.3
  191.9 0.1 copy.49
  192.2 1.0 constant_dynamic-slice_fusion.3
  193.2 0.1 copy.49
  193.5 1.0 constant_dynamic-slice_fusion.3
  194.4 0.1 copy.49
  194.7 1.0 constant_dynamic-slice_fusion.3
  196.0 1.0 constant_dynamic-slice_fusion.3
  197.2 1.0 constant_dynamic-slice_fusion.3
  198.5 1.0 constant_dynamic-slice_fusion.3
  199.8 0.1 fusion.33
  199.9 0.3 multiply_reduce_fusion.2
  200.3 1.9 convolution_convert_fusion.5
  (70 shorter events, 1.9 us)
Async XLA Ops:
  7.2 62.4 %copy-start = (bf16[2048,512]{1,0:T(8,128)(2,1)S(1)}, bf16[2048,512]{1,0:T(8,128)(2,1)}, u32[]{:S(2)}) copy-start(bf16[2048,512]{1,0:T(8,128)(2,1)} %param.31) | copy-start | bytes 6291460
  7.2 9.6 %copy-start.1 = (s32[512]{0:T(512)S(1)}, s32[512]{0:T(512)}, u32[]{:S(2)}) copy-start(s32[512]{0:T(512)} %param.23) | copy-start | bytes 6148
  7.2 106.1 %all-gather.6.cloned.1.call-start = ((), (), s32[]{:S(2)}) async-start(), calls=%async_computation | async-start | bytes 1572864 | tf_op jit(solution)/shard_map/all_gather | solution.py:160
  8.1 19.3 %copy-start.2 = (s32[512]{0:T(512)S(1)}, s32[512]{0:T(512)}, u32[]{:S(2)}) copy-start(s32[512]{0:T(512)} %param.24) | copy-start | bytes 6148
  11.2 22.2 %collective-permute-start = (bf16[512,512]{1,0:T(8,128)(2,1)S(1)}, bf16[512,512]{1,0:T(8,128)(2,1)}, u32[]{:S(2)}, u32[]{:S(2)}) collective-permute-start(bf16[512,512]{1,0:T(8,128)(2,1)S(1)} %gather_fusion), channel_id=1, source_target_pairs={{0,1},{1,2},{2,3},{3,4},{4,5},{5,6},{6,7},{7,8},{8,9},{9,10},{10,1... | collective-permute-start | bytes 1572872 | tf_op jit(solution)/shard_map/ppermute | solution.py:20
  11.7 22.8 %collective-permute-start.1 = (bf16[512,512]{1,0:T(8,128)(2,1)S(1)}, bf16[512,512]{1,0:T(8,128)(2,1)}, u32[]{:S(2)}, u32[]{:S(2)}) collective-permute-start(bf16[512,512]{1,0:T(8,128)(2,1)S(1)} %gather_fusion), channel_id=1, source_target_pairs={{1,0},{2,1},{3,2},{4,3},{5,4},{6,5},{7,6},{8,7},{9,8},{10,9},{11,1... | collective-permute-start | bytes 1572872 | tf_op jit(solution)/shard_map/ppermute | solution.py:22
  20.3 10.5 %collective-permute-start.2 = (bf16[512]{0:T(512)(128)(2,1)S(1)}, bf16[512]{0:T(512)(128)(2,1)S(1)}, u32[]{:S(2)}, u32[]{:S(2)}) collective-permute-start(bf16[512]{0:T(512)(128)(2,1)S(1)} %convert_element_type.70), channel_id=1, source_target_pairs={{0,1},{1,2},{2,3},{3,4},{4,5},{5,6},{6,7},{7,8},{8,9},{9,10},{10,1... | collective-permute-start | bytes 3080 | tf_op jit(solution)/shard_map/ppermute | solution.py:20
  20.4 10.5 %collective-permute-start.3 = (bf16[512]{0:T(512)(128)(2,1)S(1)}, bf16[512]{0:T(512)(128)(2,1)S(1)}, u32[]{:S(2)}, u32[]{:S(2)}) collective-permute-start(bf16[512]{0:T(512)(128)(2,1)S(1)} %convert_element_type.70), channel_id=1, source_target_pairs={{1,0},{2,1},{3,2},{4,3},{5,4},{6,5},{7,6},{8,7},{9,8},{10,9},{11,1... | collective-permute-start | bytes 3080 | tf_op jit(solution)/shard_map/ppermute | solution.py:22
  30.9 8.1 %copy-start.11 = (bf16[512,512]{1,0:T(8,128)(2,1)S(1)}, bf16[512,512]{1,0:T(8,128)(2,1)}, u32[]{:S(2)}) copy-start(bf16[512,512]{1,0:T(8,128)(2,1)} %param.27) | copy-start | bytes 1572868
  35.6 5.5 %copy-start.4 = (pred[512,1536]{1,0:T(8,128)(4,1)S(1)}, pred[512,1536]{1,0:T(8,128)(4,1)}, u32[]{:S(2)}) copy-start(pred[512,1536]{1,0:T(8,128)(4,1)} %fusion.21) | copy-start | bytes 2359300
  57.1 11.0 %copy-start.7 = (bf16[512,512]{1,0:T(8,128)(2,1)S(1)}, bf16[512,512]{1,0:T(8,128)(2,1)}, u32[]{:S(2)}) copy-start(bf16[512,512]{1,0:T(8,128)(2,1)} %param.28) | copy-start | bytes 1572868
  57.1 12.5 %copy-start.12 = (f32[512]{0:T(512)S(1)}, f32[512]{0:T(512)}, u32[]{:S(2)}) copy-start(f32[512]{0:T(512)} %param.29) | copy-start | bytes 6148
  69.6 6.4 %copy-start.9 = (f32[512]{0:T(512)S(1)}, f32[512]{0:T(512)}, u32[]{:S(2)}) copy-start(f32[512]{0:T(512)} %param.32) | copy-start | bytes 6148
  76.0 6.5 %copy-start.6 = (bf16[512,512]{1,0:T(8,128)(2,1)S(1)}, bf16[512,512]{1,0:T(8,128)(2,1)}, u32[]{:S(2)}) copy-start(bf16[512,512]{1,0:T(8,128)(2,1)} %param.34) | copy-start | bytes 1572868
  76.0 6.5 %copy-start.8 = (bf16[16,512]{1,0:T(8,128)(2,1)S(1)}, bf16[16,512]{1,0:T(8,128)(2,1)}, u32[]{:S(2)}) copy-start(bf16[16,512]{1,0:T(8,128)(2,1)} %param.33) | copy-start | bytes 49156
  77.4 35.9 %copy-start.3 = (bf16[512,512]{0,1:T(8,128)(2,1)}, bf16[512,512]{0,1:T(8,128)(2,1)S(1)}, u32[]{:S(2)}) copy-start(bf16[512,512]{0,1:T(8,128)(2,1)S(1)} %multiply_convert_fusion) | copy-start | bytes 1572868
  80.0 37.6 %all-gather.8.cloned.1.call-start = ((), (), s32[]{:S(2)}) async-start(), calls=%async_computation.1 | async-start | bytes 1572864 | tf_op jit(solution)/shard_map/all_gather | solution.py:161
  82.4 107.3 %all-gather.10.cloned.1.call-start = ((), (), s32[]{:S(2)}) async-start(), calls=%async_computation.2 | async-start | bytes 2359296 | tf_op jit(solution)/shard_map/all_gather | solution.py:30
  190.8 9.1 %copy-start.5 = (bf16[512,512]{1,0:T(8,128)(2,1)S(1)}, bf16[512,512]{1,0:T(8,128)(2,1)}, u32[]{:S(2)}) copy-start(bf16[512,512]{1,0:T(8,128)(2,1)} %param.37) | copy-start | bytes 1572868
  190.9 9.4 %copy-start.10 = (f32[512]{0:T(512)S(1)}, f32[512]{0:T(512)}, u32[]{:S(2)}) copy-start(f32[512]{0:T(512)} %param.38) | copy-start | bytes 6148
Sparse Core Ops, SparseCore 0:
  80.1 6.6 all-gather.5
  88.3 10.1 all-gather.7
  123.1 47.2 all-gather.9
where the time goes:
time: 210 us; the launch traced here: 209 us
  blocking collectives  92.3 us (44%)
  matrix products  55.6 us (26%)
  local copies, waits for them, and re-layouts  27.4 us (13%)
  between operations  14.1 us (7%)
  starting transfers between devices  10.2 us (5%)
  other arithmetic  8.66 us (4%)
    all_gather x2, blocking collectives, joined(): everything = jax.tree.map(lambda part: lax.all_gather(part, axis), value)  61.8 us
    all_gather x1, blocking collectives, on_device(): all_queries = lax.all_gather(local_queries, 'hit', axis=0, tiled=True)  30.5 us
    sub x1, matrix products, band_attention(): expo = jnp.where(allowed[None], jnp.exp(scores - peak), 0.0)  16 us
    dot_general x6, matrix products, project(): jnp.dot(rows, weight, preferred_element_type=jnp.float32)  12.8 us
    dot_general x1, matrix products, band_attention(): jnp.einsum('hqk,khd->qhd', probs, value_heads, preferred_element_type=jnp...  11 us
    ppermute x2, starting transfers between devices, padded(): lax.ppermute(head, axis, [((i + 1) % count, i) for i in range(count)])  9.48 us
    dynamic_slice x14, local copies, waits for them, and re-layouts, lap(): return combine(so_far, jax.tree.map(lambda part: part[k], everything))  7.72 us
    dot_general x1, matrix products, encoder_tail(): jnp.dot(hidden, ffn_down, preferred_element_type=jnp.float32)  6.36 us
  transfers between devices with their start and end apart: 7, of which 0 were waited for; matrix products, arithmetic and copies ran while one was open for 12% of the time, Pallas kernels for 0%

commit v1 on v0

v1 whole, which is shorter than its diff:
```python
import functools
import math

import jax
import jax.numpy as jnp
from jax import lax
from jax.experimental import pallas as pl
from jax.experimental.pallas import tpu as pltpu
from jax.sharding import PartitionSpec as P

HEADS = 8
LANES = 128
SUBLANES = 16
EPS = 1e-05
MASKED = -1e30
LOG2E = math.log2(math.e)
F32 = jnp.float32
BF16 = jnp.bfloat16
NN = (((1,), (0,)), ((), ()))
NT = (((1,), (1,)), ((), ()))


def dot(a, b, dims=NN):
    return lax.dot_general(a, b, dims, preferred_element_type=F32)


def rms(values, gain):
    scale = lax.rsqrt(jnp.mean(values * values, axis=-1, keepdims=True) + EPS)
    return values * scale * gain


def lane_of(shape):
    return lax.broadcasted_iota(jnp.int32, shape, len(shape) - 1)


def row_of(shape):
    return lax.broadcasted_iota(jnp.int32, shape, len(shape) - 2)


def sort_body(hits, order, valid, reach, payload, reach_out):
    count = hits.shape[0]
    wide = jnp.broadcast_to(order[...].astype(F32), (LANES, count))
    place = jnp.concatenate(
        [wide[:, c : c + LANES].T for c in range(0, count, LANES)], axis=0
    ).astype(jnp.int32)
    parts = []
    reaches = jnp.zeros((count, 1), F32)
    for c in range(0, count, LANES):
        hot = place == lane_of((count, LANES)) + c
        parts.append(jnp.where(hot, 1.0, 0.0).astype(BF16))
        reaches += jnp.sum(
            jnp.where(hot, reach[:, c : c + LANES].astype(F32), 0.0), axis=1, keepdims=True
        )
    moves = jnp.concatenate(parts, axis=1)
    payload[:count, :] = dot(moves, hits[...]).astype(BF16)
    flags = jnp.broadcast_to(valid[...].astype(F32), (SUBLANES, count)).astype(BF16)
    payload[count:, :] = dot(flags, moves, NT).astype(BF16)
    reach_out[...] = jnp.broadcast_to(reaches, (count, LANES))


def head_lanes(shape, head):
    lane = lane_of(shape)
    half = shape[-1] // 2
    return lane < half if head % 2 == 0 else lane >= half


def bias_tile(rows, cols, row0, col0, reach, valid, shift, own):
    offset = (lane_of((rows, cols)) + (col0 + shift)) - (row_of((rows, cols)) + row0)
    near = jnp.abs(offset).astype(F32) <= reach
    seen = valid > 0.5
    if own:
        seen = seen | (offset == 0)
    return jnp.where(near & seen, 0.0, MASKED)


def softmax_parts(scores):
    peak = functools.reduce(
        jnp.maximum, [jnp.max(s, axis=1, keepdims=True) for s in scores]
    )
    return peak, [jnp.exp2(s - peak).astype(BF16) for s in scores]


def pair_attend(query, blocks):
    outs, peaks = [], []
    for head in range(2):
        mine = jnp.where(head_lanes(query.shape, head), query, jnp.zeros_like(query))
        scores = []
        for keys, _, bias in blocks:
            s = dot(mine, keys, NT)
            scores.append(s if bias is None else s + bias)
        peak, weights = softmax_parts(scores)
        total = None
        for w, (_, values, _) in zip(weights, blocks):
            held = jnp.where(head_lanes(values.shape, head), values, jnp.ones_like(values))
            part = dot(w, held)
            total = part if total is None else total + part
        outs.append(total)
        peaks.append(peak)
    low = head_lanes(outs[0].shape, 0)
    output = jnp.where(low, outs[0], outs[1])
    total = pltpu.roll(jnp.where(low, outs[1], outs[0]), outs[0].shape[1] // 2, 1)
    return output, total, peaks


def local_body(
    side, own, other, reach, wq, wk, wv, q_out, out, total, peak, keys, values, bias
):
    count = reach.shape[0]
    tile = count // 2
    right = side[0] == 0
    hits = own[:count, :]
    scale = LOG2E / math.sqrt(hits.shape[1] // HEADS)
    q_out[...] = (dot(hits, wq[...]) * scale).astype(BF16)
    keys[:count, :] = dot(hits, wk[...]).astype(BF16)
    values[:count, :] = dot(hits, wv[...]).astype(BF16)
    next_hits = other[:count, :]
    keys[count:, :] = dot(next_hits, wk[...]).astype(BF16)
    values[count:, :] = dot(next_hits, wv[...]).astype(BF16)
    shift = jnp.where(right, count, -count)
    own_valid = own[count : count + 1, :].astype(F32)
    other_valid = other[count : count + 1, :].astype(F32)
    bias[:, :count] = bias_tile(count, count, 0, 0, reach[:, :1], own_valid, 0, True)
    bias[:, count:] = bias_tile(count, count, 0, 0, reach[:, :1], other_valid, shift, False)
    peak[...] = jnp.zeros_like(peak)

    heavy = pl.multiple_of(jnp.where(right, tile, 0), tile)
    light = pl.multiple_of(jnp.where(right, 0, tile), tile)

    def tile_of(start, cols, first, width):
        rows = pl.ds(start, tile)
        blocks = [(keys[:count, cols], values[:count, cols], bias[rows, :count])]
        if width == count:
            blocks.append((keys[count:, cols], values[count:, cols], bias[rows, count:]))
        else:
            part = pl.ds(pl.multiple_of(count + first, tile), width)
            half = jnp.where(right, bias[rows, count : count + tile], bias[rows, count + tile :])
            blocks.append((keys[part, cols], values[part, cols], half))
        return pair_attend(q_out[rows, cols], blocks)

    for pair in range(HEADS // 2):
        cols = slice(pair * LANES, (pair + 1) * LANES)
        for start, width in ((heavy, count), (light, tile)):
            rows = pl.ds(start, tile)
            o, t, p = tile_of(start, cols, light, width)
            out[rows, cols] = o
            total[rows, cols] = t
            lane = lane_of((tile, LANES))
            now = peak[rows, :]
            for head in range(2):
                now = jnp.where(lane == 2 * pair + head, p[head], now)
            peak[rows, :] = now


def rest_body(
    side, own, other, reach, query, out1, total1, peak1, wk, wv, wo, gain1, up, down, gain2,
    encoded, keys, values, bias, context,
):
    count = reach.shape[0]
    tile = count // 2
    right = side[0] == 1
    hits = other[:count, :]
    keys[...] = dot(hits, wk[...]).astype(BF16)
    values[...] = dot(hits, wv[...]).astype(BF16)
    shift = jnp.where(right, count, -count)
    valid = other[count : count + 1, :].astype(F32)
    bias[...] = bias_tile(count, count, 0, 0, reach[:, :1], valid, shift, False)
    heavy = pl.multiple_of(jnp.where(right, tile, 0), tile)
    light = pl.multiple_of(jnp.where(right, 0, tile), tile)
    for pair in range(HEADS // 2):
        cols = slice(pair * LANES, (pair + 1) * LANES)
        for start, width in ((heavy, count), (light, tile)):
            rows = pl.ds(start, tile)
            if width == count:
                block = (keys[:, cols], values[:, cols], bias[rows, :])
            else:
                part = pl.ds(light, tile)
                half = jnp.where(right, bias[rows, :tile], bias[rows, tile:])
                block = (keys[part, cols], values[part, cols], half)
            o, t, p = pair_attend(query[rows, cols], [block])
            low = head_lanes(o.shape, 0)
            before, after = [], []
            for head in range(2):
                col = 2 * pair + head
                old = peak1[rows, col : col + 1]
                top = jnp.maximum(old, p[head])
                before.append(jnp.exp2(old - top))
                after.append(jnp.exp2(p[head] - top))
            b = jnp.where(low, before[0], before[1])
            a = jnp.where(low, after[0], after[1])
            whole = total1[rows, cols] * b + t * a
            context[rows, cols] = ((out1[rows, cols] * b + o * a) / whole).astype(BF16)
    middle = rms(dot(context[...], wo[...]) + own[:count, :].astype(F32), gain1[...]).astype(BF16)
    width = hits.shape[1]
    total = middle.astype(F32)
    for c in range(0, up.shape[1], width):
        hidden = jax.nn.gelu(dot(middle, up[:, c : c + width]), approximate=True).astype(BF16)
        total += dot(hidden, down[c : c + width, :])
    encoded[...] = rms(total, gain2[...]).astype(BF16)


def split3(value):
    high = value.astype(BF16)
    left = value - high.astype(F32)
    mid = left.astype(BF16)
    return high, mid, (left - mid.astype(F32)).astype(BF16)


def decode_own_body(enc, queries, wq, wk, wv, dq, out, total, peak):
    scale = LOG2E / math.sqrt(enc.shape[1] // HEADS)
    dq[...] = (dot(queries[...], wq[...]) * scale).astype(BF16)
    keys = dot(enc[...], wk[...]).astype(BF16)
    values = dot(enc[...], wv[...]).astype(BF16)
    lane = lane_of(peak.shape)
    now = jnp.zeros(peak.shape, F32)
    for pair in range(HEADS // 2):
        cols = slice(pair * LANES, (pair + 1) * LANES)
        o, t, p = pair_attend(dq[:, cols], [(keys[:, cols], values[:, cols], None)])
        out[:, cols] = o
        total[:, cols] = t
        for head in range(2):
            now = jnp.where(lane == 2 * pair + head, p[head], now)
    peak[...] = now


def decode_other_body(enc, dq, out1, total1, peak1, wk, wv, payload):
    keys = dot(enc[...], wk[...]).astype(BF16)
    values = dot(enc[...], wv[...]).astype(BF16)
    width = enc.shape[1]
    lane = lane_of(peak1.shape)
    tops = jnp.zeros(peak1.shape, F32)
    sums = jnp.zeros(peak1.shape, F32)
    for pair in range(HEADS // 2):
        cols = slice(pair * LANES, (pair + 1) * LANES)
        o, t, p = pair_attend(dq[:, cols], [(keys[:, cols], values[:, cols], None)])
        low = head_lanes(o.shape, 0)
        before, after = [], []
        for head in range(2):
            col = 2 * pair + head
            old = peak1[:, col : col + 1]
            top = jnp.maximum(old, p[head])
            before.append(jnp.exp2(old - top))
            after.append(jnp.exp2(p[head] - top))
            tops = jnp.where(lane == col, top, tops)
        b = jnp.where(low, before[0], before[1])
        a = jnp.where(low, after[0], after[1])
        whole = total1[:, cols] * b + t * a
        payload[:, cols] = ((out1[:, cols] * b + o * a) / whole).astype(BF16)
        half = LANES // 2
        for head in range(2):
            sums = jnp.where(
                lane == 2 * pair + head, whole[:, head * half : head * half + 1], sums
            )
    pieces = split3(tops) + split3(sums)
    packed = jnp.zeros(peak1.shape, F32)
    for i, piece in enumerate(pieces):
        value = piece.astype(F32)
        moved = pltpu.roll(value, i * HEADS, 1) if i else value
        packed = jnp.where((lane >= i * HEADS) & (lane < (i + 1) * HEADS), moved, packed)
    payload[:, width:] = packed.astype(BF16)


def merge_body(parts, objects, wo, gain, proj, decoded):
    spans, owned, _ = parts.shape
    width = objects.shape[1]
    each = width // HEADS
    tops, sums = [], []
    for s in range(spans):
        extra = parts[s, :, width:].astype(F32)
        cut = [extra[:, i * HEADS : (i + 1) * HEADS] for i in range(6)]
        tops.append(cut[0] + cut[1] + cut[2])
        sums.append(cut[3] + cut[4] + cut[5])
    top = functools.reduce(jnp.maximum, tops)
    shares = [t * jnp.exp2(p - top) for t, p in zip(sums, tops)]
    denom = functools.reduce(jnp.add, shares)
    numer = jnp.zeros((owned, width), F32)
    half = LANES // 2
    for s in range(spans):
        share = shares[s] / denom
        spread = jnp.concatenate(
            [jnp.broadcast_to(share[:, h : h + 1], (owned, each)) for h in range(HEADS)], axis=1
        )
        numer += parts[s, :, :width].astype(F32) * spread
    cross = numer.astype(BF16)
    normed = rms(dot(cross, wo[...]) + objects[...].astype(F32), gain[...]).astype(BF16)
    decoded[...] = dot(normed, proj[...]).astype(BF16)


def scratch_call(body, outs, scratch, operands, flops, moved, name):
    vmem = pl.BlockSpec(memory_space=pltpu.VMEM)
    smem = pl.BlockSpec(memory_space=pltpu.SMEM)
    specs = [smem if x.ndim == 1 else vmem for x in operands]
    return pl.pallas_call(
        body,
        out_shape=outs,
        in_specs=specs,
        out_specs=[vmem] * len(outs),
        scratch_shapes=scratch,
        compiler_params=pltpu.CompilerParams(vmem_limit_bytes=60 * 1024 * 1024),
        cost_estimate=pl.CostEstimate(flops=flops, bytes_accessed=moved, transcendentals=0),
        name=name,
    )(*operands)


def shape(dims, dtype):
    return jax.ShapeDtypeStruct(dims, dtype)


def on_device(
    hits, order, valid, reach,
    enc_wq, enc_wk, enc_wv, enc_wo, enc_gain1, ffn_up, ffn_down, enc_gain2,
    object_queries, dec_wq, dec_wk, dec_wv, dec_wo, dec_gain, out_proj,
):
    count, width = hits.shape
    owned = object_queries.shape[0]
    spans = lax.axis_size("hit")
    ring = lax.axis_size(("hit", "query"))
    cube = 2 * count * width * width

    swap = [(i, i ^ 1) for i in range(ring)]
    beyond = [(i, (i + 1) % ring if i % 2 else (i - 1) % ring) for i in range(ring)]
    side = lax.axis_index("query").astype(jnp.int32).reshape(1)

    gathered = lax.all_to_all(
        jnp.broadcast_to(object_queries[None], (spans, owned, width)), "hit", 0, 0
    ).reshape(spans * owned, width)

    payload, reach_rows = scratch_call(
        sort_body,
        [shape((count + SUBLANES, width), BF16), shape((count, LANES), F32)],
        [],
        [hits, order, valid[None], reach[None]],
        cube,
        2 * count * width * 2,
        "sort_hits",
    )
    far = lax.ppermute(payload, ("hit", "query"), beyond)
    near = lax.ppermute(payload, ("hit", "query"), swap)
    query, out1, total1, peak1 = scratch_call(
        local_body,
        [
            shape((count, width), BF16),
            shape((count, width), F32),
            shape((count, width), F32),
            shape((count, LANES), F32),
        ],
        [
            pltpu.VMEM((2 * count, width), BF16),
            pltpu.VMEM((2 * count, width), BF16),
            pltpu.VMEM((count, 2 * count), F32),
        ],
        [side, payload, near, reach_rows, enc_wq, enc_wk, enc_wv],
        20 * cube,
        16 * count * width,
        "attend_chip",
    )
    (encoded,) = scratch_call(
        rest_body,
        [shape((count, width), BF16)],
        [
            pltpu.VMEM((count, width), BF16),
            pltpu.VMEM((count, width), BF16),
            pltpu.VMEM((count, count), F32),
            pltpu.VMEM((count, width), BF16),
        ],
        [
            side, payload, far, reach_rows, query, out1, total1, peak1,
            enc_wk, enc_wv, enc_wo, enc_gain1[None], ffn_up, ffn_down, enc_gain2[None],
        ],
        20 * cube,
        30 * count * width,
        "attend_far",
    )
    partner = lax.ppermute(encoded, ("hit", "query"), swap)
    rows = spans * owned
    dq, dout, dtotal, dpeak = scratch_call(
        decode_own_body,
        [
            shape((rows, width), BF16),
            shape((rows, width), F32),
            shape((rows, width), F32),
            shape((rows, LANES), F32),
        ],
        [],
        [encoded, gathered, dec_wq, dec_wk, dec_wv],
        4 * cube,
        8 * count * width,
        "decode_own",
    )
    (parts,) = scratch_call(
        decode_other_body,
        [shape((rows, width + LANES), BF16)],
        [],
        [partner, dq, dout, dtotal, dpeak, dec_wk, dec_wv],
        4 * cube,
        8 * count * width,
        "decode_other",
    )
    exchanged = lax.all_to_all(parts.reshape(spans, owned, width + LANES), "hit", 0, 0)
    (decoded,) = scratch_call(
        merge_body,
        [shape((owned, width), BF16)],
        [],
        [exchanged, object_queries, dec_wo, dec_gain[None], out_proj],
        4 * owned * width * width,
        4 * width * width,
        "merge_spans",
    )
    return (encoded, decoded)


def solution(mesh):
    split = P(("groups", "hit", "query"), None)
    flat = P(("groups", "hit", "query"))
    same = P()
    in_specs = (
        split, split, flat, flat,
        same, same, same, same, same, same, same, same,
        split,
        same, same, same, same, same, same,
    )
    return jax.shard_map(
        on_device, mesh=mesh, in_specs=in_specs, out_specs=(split, split), check_vma=False
    )
```

time: 210 us -> 74.1 us (0.35)
  blocking collectives: 92.3 us -> 22.5 us
  matrix products: 55.6 us -> 0 us
  Pallas kernels: 0 us -> 41.9 us
  local copies, waits for them, and re-layouts: 27.4 us -> 2.43 us
  between operations: 14.1 us -> 0.66 us
  other arithmetic: 8.66 us -> 0 us
  starting transfers between devices: 10.2 us -> 6.15 us
    all_gather x3 -> x0, blocking collectives: 92.3 us -> none  [the longest x2 61.8 us: joined(): everything = jax.tree.map(lambda part: lax.all_gather(part, axis), value)]
    pallas_call x0 -> x6, Pallas kernels: none -> 41.9 us  [scratch_call(): pl.pallas_call(body, out_shape=outs, in_specs=specs, out_specs=[vmem] * l...]
    dot_general x13 -> x0, matrix products: 39.7 us -> none  [the longest x6 12.8 us: project(): jnp.dot(rows, weight, preferred_element_type=jnp.float32)]
    all_to_all x0 -> x2, blocking collectives: none -> 22.5 us  [the longest x1 11.6 us: on_device(): lax.all_to_all(parts.reshape(spans, owned, width + LANES), 'hit', 0, 0)]
    sub x1 -> x0, matrix products: 16 us -> none  [band_attention(): expo = jnp.where(allowed[None], jnp.exp(scores - peak), 0.0)]
    gather x4 -> x0, local copies, waits for them, and re-layouts: 10.3 us -> none  [the longest x1 3.49 us: on_device(): sorted_reach = reach[place]]
    dynamic_slice x15 -> x0, local copies, waits for them, and re-layouts: 7.8 us -> none  [the longest x14 7.72 us: lap(): return combine(so_far, jax.tree.map(lambda part: part[k], everything))]
    ppermute x4 -> x3, starting transfers between devices: 10.1 us -> 6.15 us  [the longest x1 5.66 us: on_device(): far = lax.ppermute(payload, ('hit', 'query'), beyond)]
  transfers between devices with their start and end apart: 7 -> 3, of which waited for: 0 -> 0; matrix products, arithmetic and copies ran while one was open for 12% -> 0% of each run, Pallas kernels for 0% -> 23%
where the time goes in v1:
time: 74.1 us; the launch traced here: 73.7 us
  Pallas kernels  41.9 us (57%)
  blocking collectives  22.5 us (30%)
  starting transfers between devices  6.15 us (8%)
  local copies, waits for them, and re-layouts  2.43 us (3%)
    pallas_call x6, Pallas kernels, scratch_call(): pl.pallas_call(body, out_shape=outs, in_specs=specs, out_specs=[vmem] * l...  41.9 us
    all_to_all x1, blocking collectives, on_device(): lax.all_to_all(parts.reshape(spans, owned, width + LANES), 'hit', 0, 0)  11.6 us
    all_to_all x1, blocking collectives, on_device(): lax.all_to_all(jnp.broadcast_to(object_queries[None], (spans, owned, widt...  11 us
    ppermute x1, starting transfers between devices, on_device(): far = lax.ppermute(payload, ('hit', 'query'), beyond)  5.66 us
    unnamed x8, local copies, waits for them, and re-layouts  2.42 us
  transfers between devices with their start and end apart: 3, of which 0 were waited for; matrix products, arithmetic and copies ran while one was open for 0% of the time, Pallas kernels for 23%

profile of v1, /device:TPU:0, one launch (start us, length us, event | category | flops | bytes accessed | tf_op | source)
XLA Modules:
  0.0 73.7 jit_solution(4546700376720304414)
XLA Ops:
  0.6 2.5 %sort_hits.1 = (bf16[528,512]{1,0:T(8,128)(2,1)}, f32[512,128]{1,0:T(8,128)}) custom-call(bf16[512,512]{1,0:T(8,128)(2,1)} %hits.1, s32[1,512]{1,0:T(1,128)} %order.1, s32[1,512]{1,0:T(1,128)} %bitcast.11, s32[1,512]{1,0:T(1,128)} %bitcast.12), custom_call_target="tpu_custom_call" | custom-call | flops 268435456 | bytes 1048576 | tf_op jit(solution)/shard_map/sort_hits/pallas_call | solution.py:292
  3.1 0.5 collective-permute-start.1
  3.6 5.7 %collective-permute-start = (bf16[528,512]{1,0:T(8,128)(2,1)}, bf16[528,512]{1,0:T(8,128)(2,1)S(1)}, u32[]{:S(2)}, u32[]{:S(2)}) collective-permute-start(bf16[528,512]{1,0:T(8,128)(2,1)} %get-tuple-element.12.own), channel_id=1, source_target_pairs={{0,15},{1,2},{2,1},{3,4},{4,3},{5,6},{6,5},{7,8},{8,7},{9,10},{10,... | collective-permute-start | bytes 1622024 | tf_op jit(solution)/shard_map/ppermute | solution.py:336
  9.3 0.0 collective-permute-done.1.other
  9.3 0.0 copy-start.2
  9.3 0.8 %copy-done.2 = bf16[528,512]{1,0:T(8,128)(2,1)} copy-done((bf16[528,512]{1,0:T(8,128)(2,1)}, bf16[528,512]{1,0:T(8,128)(2,1)S(1)}, u32[]{:S(2)}) %copy-start.2) | copy-done | bytes 540696
  10.1 11.8 %attend_chip.1 = (bf16[512,512]{1,0:T(8,128)(2,1)}, f32[512,512]{1,0:T(8,128)}, f32[512,512]{1,0:T(8,128)}, f32[512,128]{1,0:T(8,128)}) custom-call(s32[1]{0:T(128)} %bitcast.side, bf16[528,512]{1,0:T(8,128)(2,1)} %get-tuple-element.12.own, bf16[528,512]{1,0:T(8,128)(2,1)} %copy-done.2, f32[512,128]{1,0:T(8,128)} %get-tuple-element.13.reach, ...), custom_call_target="tpu_custom_call" | custom-call | flops 5368709120 | bytes 4194304 | tf_op jit(solution)/shard_map/attend_chip/pallas_call | solution.py:292
  21.9 0.0 collective-permute-done.other
  21.9 0.0 copy-start.1
  21.9 0.8 %copy-done.1 = bf16[528,512]{1,0:T(8,128)(2,1)} copy-done((bf16[528,512]{1,0:T(8,128)(2,1)}, bf16[528,512]{1,0:T(8,128)(2,1)S(1)}, u32[]{:S(2)}) %copy-start.1) | copy-done | bytes 540696
  22.7 0.0 copy-start
  22.7 14.2 %attend_far.1.enc = bf16[512,512]{1,0:T(8,128)(2,1)} custom-call(s32[1]{0:T(128)} %bitcast.side, bf16[528,512]{1,0:T(8,128)(2,1)} %get-tuple-element.12.own, bf16[528,512]{1,0:T(8,128)(2,1)} %copy-done.1, f32[512,128]{1,0:T(8,128)} %get-tuple-element.13.reach, bf16[512,512]{1,0:T(8,128)(2,1)} %get-tuple-element.14.query, f32[512,512]{1,0:T(8,128)} %get-tuple-element.15.out1, ...), custom_call_target="tpu_custom_call" | custom-call | flops 5368709120 | bytes 7864320 | tf_op jit(solution)/shard_map/attend_far/pallas_call | solution.py:292
  36.9 0.0 collective-permute-start.2
  36.9 0.0 copy-done
  36.9 11.0 %all_to_all.10 = bf16[8,16,512]{2,1,0:T(8,128)(2,1)} all-to-all(bf16[8,16,512]{2,1,0:T(8,128)(2,1)S(1)} %broadcast_in_dim.25), channel_id=1, replica_groups=mesh['groups'=2,'hit'=8,'query'=2] {'hit'}, dimensions={0} | all-to-all | bytes 262144 | tf_op jit(solution)/shard_map/all_to_all | solution.py:323
  47.9 5.2 %decode_own.1 = (bf16[128,512]{1,0:T(8,128)(2,1)}, f32[128,512]{1,0:T(8,128)}, f32[128,512]{1,0:T(8,128)}, f32[128,128]{1,0:T(8,128)}) custom-call(bf16[512,512]{1,0:T(8,128)(2,1)} %attend_far.1.enc, bf16[128,512]{1,0:T(8,128)(2,1)} %bitcast.9, bf16[512,512]{1,0:T(8,128)(2,1)} %wq.3, bf16[512,512]{1,0:T(8,128)(2,1)} %wk.7, bf16[512,512]{1,0:T(8,128)(2,1)} %wv.7), custom_call_target="tpu_custom_call" | custom-call | flops 1073741824 | bytes 2097152 | tf_op jit(solution)/shard_map/decode_own/pallas_call | solution.py:292
  53.1 0.0 collective-permute-done.2.enc
  53.1 0.0 copy-start.3
  53.1 0.8 %copy-done.3 = bf16[512,512]{1,0:T(8,128)(2,1)} copy-done((bf16[512,512]{1,0:T(8,128)(2,1)}, bf16[512,512]{1,0:T(8,128)(2,1)S(1)}, u32[]{:S(2)}) %copy-start.3) | copy-done | bytes 524312
  53.9 5.4 %decode_other.1 = bf16[128,640]{1,0:T(8,128)(2,1)} custom-call(bf16[512,512]{1,0:T(8,128)(2,1)} %copy-done.3, bf16[128,512]{1,0:T(8,128)(2,1)} %get-tuple-element.18.dq, f32[128,512]{1,0:T(8,128)} %get-tuple-element.19.out1, f32[128,512]{1,0:T(8,128)} %get-tuple-element.20.total1, f32[128,128]{1,0:T(8,128)} %get-tuple-element.21.peak1, bf16[512,512]{1,0:T(8,128)(2,1)} %wk.7, ...), custom_call_target="tpu_custom_call" | custom-call | flops 1073741824 | bytes 2097152 | tf_op jit(solution)/shard_map/decode_other/pallas_call | solution.py:292
  59.4 11.6 %all_to_all.11.parts = bf16[8,16,640]{2,1,0:T(8,128)(2,1)} all-to-all(bf16[8,16,640]{2,1,0:T(8,128)(2,1)} %bitcast.8), channel_id=1, replica_groups=mesh['groups'=2,'hit'=8,'query'=2] {'hit'}, dimensions={0} | all-to-all | bytes 327680 | tf_op jit(solution)/shard_map/all_to_all | solution.py:398
  70.9 2.7 %merge_spans.1 = bf16[16,512]{1,0:T(8,128)(2,1)} custom-call(bf16[8,16,640]{2,1,0:T(8,128)(2,1)} %all_to_all.11.parts, bf16[16,512]{1,0:T(8,128)(2,1)} %objects.1, bf16[512,512]{1,0:T(8,128)(2,1)} %wo.3, f32[1,512]{1,0:T(1,128)} %bitcast.10, bf16[512,512]{1,0:T(8,128)(2,1)} %proj.1), custom_call_target="tpu_custom_call" | custom-call | flops 16777216 | bytes 1048576 | tf_op jit(solution)/shard_map/merge_spans/pallas_call | solution.py:292
  (1 shorter events, 0.0 us)
Async XLA Ops:
  3.1 6.2 %collective-permute-start.1 = (bf16[528,512]{1,0:T(8,128)(2,1)}, bf16[528,512]{1,0:T(8,128)(2,1)S(1)}, u32[]{:S(2)}, u32[]{:S(2)}) collective-permute-start(bf16[528,512]{1,0:T(8,128)(2,1)} %get-tuple-element.12.own), channel_id=1, source_target_pairs={{0,1},{1,0},{2,3},{3,2},{4,5},{5,4},{6,7},{7,6},{8,9},{9,8},{10,11... | collective-permute-start | bytes 1622024 | tf_op jit(solution)/shard_map/ppermute | solution.py:337
  3.6 18.3 %collective-permute-start = (bf16[528,512]{1,0:T(8,128)(2,1)}, bf16[528,512]{1,0:T(8,128)(2,1)S(1)}, u32[]{:S(2)}, u32[]{:S(2)}) collective-permute-start(bf16[528,512]{1,0:T(8,128)(2,1)} %get-tuple-element.12.own), channel_id=1, source_target_pairs={{0,15},{1,2},{2,1},{3,4},{4,3},{5,6},{6,5},{7,8},{8,7},{9,10},{10,... | collective-permute-start | bytes 1622024 | tf_op jit(solution)/shard_map/ppermute | solution.py:336
  9.3 0.8 %copy-start.2 = (bf16[528,512]{1,0:T(8,128)(2,1)}, bf16[528,512]{1,0:T(8,128)(2,1)S(1)}, u32[]{:S(2)}) copy-start(bf16[528,512]{1,0:T(8,128)(2,1)S(1)} %collective-permute-done.1.other) | copy-start | bytes 1622020
  21.9 0.8 %copy-start.1 = (bf16[528,512]{1,0:T(8,128)(2,1)}, bf16[528,512]{1,0:T(8,128)(2,1)S(1)}, u32[]{:S(2)}) copy-start(bf16[528,512]{1,0:T(8,128)(2,1)S(1)} %collective-permute-done.other) | copy-start | bytes 1622020
  22.7 14.2 %copy-start = (bf16[16,512]{1,0:T(8,128)(2,1)S(1)}, bf16[16,512]{1,0:T(8,128)(2,1)}, u32[]{:S(2)}) copy-start(bf16[16,512]{1,0:T(8,128)(2,1)} %objects.1) | copy-start | bytes 49156
  36.9 16.3 %collective-permute-start.2 = (bf16[512,512]{1,0:T(8,128)(2,1)}, bf16[512,512]{1,0:T(8,128)(2,1)S(1)}, u32[]{:S(2)}, u32[]{:S(2)}) collective-permute-start(bf16[512,512]{1,0:T(8,128)(2,1)} %attend_far.1.enc), channel_id=1, source_target_pairs={{0,1},{1,0},{2,3},{3,2},{4,5},{5,4},{6,7},{7,6},{8,9},{9,8},{10,11... | collective-permute-start | bytes 1572872 | tf_op jit(solution)/shard_map/ppermute | solution.py:373
  53.1 0.8 %copy-start.3 = (bf16[512,512]{1,0:T(8,128)(2,1)}, bf16[512,512]{1,0:T(8,128)(2,1)S(1)}, u32[]{:S(2)}) copy-start(bf16[512,512]{1,0:T(8,128)(2,1)S(1)} %collective-permute-done.2.enc) | copy-start | bytes 1572868

commit v2 on v1

--- a/solution.py
+++ b/solution.py
@@ -152,9 +152,11 @@
 
 
 def rest_body(
-    side, own, other, reach, query, out1, total1, peak1, wk, wv, wo, gain1, up, down, gain2,
-    encoded, keys, values, bias, context,
+    side, own, other, reach, query, out1, total1, peak1, wk, wv, wo, gain1, up, down, gain2, objects, dec_wq,
+    encoded, dq, keys, values, bias, context,
 ):
+    scale = LOG2E / math.sqrt(own.shape[1] // HEADS)
+    dq[...] = (dot(objects[...], dec_wq[...]) * scale).astype(BF16)
     count = reach.shape[0]
     tile = count // 2
     right = side[0] == 1
@@ -205,9 +207,7 @@
     return high, mid, (left - mid.astype(F32)).astype(BF16)
 
 
-def decode_own_body(enc, queries, wq, wk, wv, dq, out, total, peak):
-    scale = LOG2E / math.sqrt(enc.shape[1] // HEADS)
-    dq[...] = (dot(queries[...], wq[...]) * scale).astype(BF16)
+def decode_own_body(enc, dq, wk, wv, out, total, peak):
     keys = dot(enc[...], wk[...]).astype(BF16)
     values = dot(enc[...], wv[...]).astype(BF16)
     lane = lane_of(peak.shape)
@@ -295,7 +295,7 @@
         in_specs=specs,
         out_specs=[vmem] * len(outs),
         scratch_shapes=scratch,
-        compiler_params=pltpu.CompilerParams(vmem_limit_bytes=60 * 1024 * 1024),
+        compiler_params=pltpu.CompilerParams(vmem_limit_bytes=24 * 1024 * 1024),
         cost_estimate=pl.CostEstimate(flops=flops, bytes_accessed=moved, transcendentals=0),
         name=name,
     )(*operands)
@@ -353,9 +353,10 @@
         16 * count * width,
         "attend_chip",
     )
-    (encoded,) = scratch_call(
+    rows = spans * owned
+    encoded, dq = scratch_call(
         rest_body,
-        [shape((count, width), BF16)],
+        [shape((count, width), BF16), shape((rows, width), BF16)],
         [
             pltpu.VMEM((count, width), BF16),
             pltpu.VMEM((count, width), BF16),
@@ -365,23 +366,22 @@
         [
             side, payload, far, reach_rows, query, out1, total1, peak1,
             enc_wk, enc_wv, enc_wo, enc_gain1[None], ffn_up, ffn_down, enc_gain2[None],
+            gathered, dec_wq,
         ],
         20 * cube,
         30 * count * width,
         "attend_far",
     )
     partner = lax.ppermute(encoded, ("hit", "query"), swap)
-    rows = spans * owned
-    dq, dout, dtotal, dpeak = scratch_call(
+    dout, dtotal, dpeak = scratch_call(
         decode_own_body,
         [
-            shape((rows, width), BF16),
             shape((rows, width), F32),
             shape((rows, width), F32),
             shape((rows, LANES), F32),
         ],
         [],
-        [encoded, gathered, dec_wq, dec_wk, dec_wv],
+        [encoded, dq, dec_wk, dec_wv],
         4 * cube,
         8 * count * width,
         "decode_own",

time: 74.1 us -> 79.2 us (1.069)
  local copies, waits for them, and re-layouts: 2.43 us -> 26.8 us
  Pallas kernels: 41.9 us -> 27.2 us
  blocking collectives: 22.5 us -> 13.8 us
  starting transfers between devices: 6.15 us -> 9.52 us
    unnamed x8 -> x70, local copies, waits for them, and re-layouts: 2.42 us -> 25.4 us
    pallas_call x6, Pallas kernels: 41.9 us -> 27.2 us  [scratch_call(): pl.pallas_call(body, out_shape=outs, in_specs=specs, out_specs=[vmem] * l...]
    all_to_all x1 -> x0, blocking collectives: 11 us -> none  [on_device(): lax.all_to_all(jnp.broadcast_to(object_queries[None], (spans, owned, widt...]
    all_to_all x0 -> x1, starting transfers between devices: none -> 3.37 us  [on_device(): lax.all_to_all(jnp.broadcast_to(object_queries[None], (spans, owned, widt...]
    all_to_all x1, blocking collectives: 11.6 us -> 13.8 us  [on_device(): lax.all_to_all(parts.reshape(spans, owned, width + LANES), 'hit', 0, 0)]
    broadcast_in_dim x1, local copies, waits for them, and re-layouts: 0.01 us -> 1.36 us  [on_device(): jnp.broadcast_to(object_queries[None], (spans, owned, width))]
  transfers between devices with their start and end apart: 3 -> 4, of which waited for: 0 -> 0; matrix products, arithmetic and copies ran while one was open for 0% -> 2% of each run, Pallas kernels for 23% -> 15%
where the time goes in v2:
time: 79.2 us; the launch traced here: 78.1 us
  Pallas kernels  27.2 us (34%)
  local copies, waits for them, and re-layouts  26.8 us (34%)
  blocking collectives  13.8 us (17%)
  starting transfers between devices  9.52 us (12%)
  between operations  0.8 us (1%)
    pallas_call x6, Pallas kernels, scratch_call(): pl.pallas_call(body, out_shape=outs, in_specs=specs, out_specs=[vmem] * l...  27.2 us
    unnamed x70, local copies, waits for them, and re-layouts  25.4 us
    all_to_all x1, blocking collectives, on_device(): lax.all_to_all(parts.reshape(spans, owned, width + LANES), 'hit', 0, 0)  13.8 us
    ppermute x1, starting transfers between devices, on_device(): far = lax.ppermute(payload, ('hit', 'query'), beyond)  5.66 us
    all_to_all x1, starting transfers between devices, on_device(): lax.all_to_all(jnp.broadcast_to(object_queries[None], (spans, owned, widt...  3.37 us
  transfers between devices with their start and end apart: 4, of which 0 were waited for; matrix products, arithmetic and copies ran while one was open for 2% of the time, Pallas kernels for 15%

profile of v2, /device:TPU:0, one launch (start us, length us, event | category | flops | bytes accessed | tf_op | source)
XLA Modules:
  0.0 78.1 jit_solution(5778973452616463368)
XLA Ops:
  0.6 1.0 %copy-done.8 = bf16[512,512]{1,0:T(8,128)(2,1)S(1)} copy-done((bf16[512,512]{1,0:T(8,128)(2,1)S(1)}, bf16[512,512]{1,0:T(8,128)(2,1)}, u32[]{:S(2)}) %copy-start.8) | copy-done | bytes 524312
  1.7 0.7 copy-done.19
  2.4 0.7 copy-done.20
  3.0 0.7 copy-done.21
  3.7 0.6 sort_hits.1
  4.3 0.7 copy-done.24
  5.0 0.5 collective-permute-start.1
  5.5 5.7 %collective-permute-start = (bf16[528,512]{1,0:T(8,128)(2,1)S(1)}, bf16[528,512]{1,0:T(8,128)(2,1)S(1)}, u32[]{:S(2)}, u32[]{:S(2)}) collective-permute-start(bf16[528,512]{1,0:T(8,128)(2,1)S(1)} %get-tuple-element.13.own), channel_id=1, source_target_pairs={{0,15},{1,2},{2,1},{3,4},{4,3},{5,6},{6,5},{7,8},{8,7},{9,10},{10,... | collective-permute-start | bytes 1622024 | tf_op jit(solution)/shard_map/ppermute | solution.py:336
  11.2 1.4 %broadcast_in_dim.25 = bf16[8,16,512]{2,1,0:T(8,128)(2,1)} broadcast(bf16[16,512]{1,0:T(8,128)(2,1)} %objects.1), dimensions={1,2} | broadcast | bytes 147456 | tf_op jit(solution)/shard_map/broadcast_in_dim | solution.py:324
  12.5 3.4 %all-to-all-start = ((bf16[8,16,512]{2,1,0:T(8,128)(2,1)}), bf16[8,16,512]{2,1,0:T(8,128)(2,1)S(1)}, u32[]{:S(2)}, u32[]{:S(2)}) async-start(bf16[8,16,512]{2,1,0:T(8,128)(2,1)} %broadcast_in_dim.25), calls=%async_computation | async-start | bytes 262144 | tf_op jit(solution)/shard_map/all_to_all | solution.py:323
  15.9 0.0 collective-permute-done.1.other
  15.9 0.8 %copy-done.6 = bf16[528,512]{1,0:T(8,128)(2,1)} copy-done((bf16[528,512]{1,0:T(8,128)(2,1)}, bf16[528,512]{1,0:T(8,128)(2,1)S(1)}, u32[]{:S(2)}) %copy-start.6) | copy-done | bytes 540696
  16.7 1.0 %copy-done.7 = bf16[528,512]{1,0:T(8,128)(2,1)S(1)} copy-done((bf16[528,512]{1,0:T(8,128)(2,1)S(1)}, bf16[528,512]{1,0:T(8,128)(2,1)}, u32[]{:S(2)}) %copy-start.7) | copy-done | bytes 540696
  17.8 1.0 %copy-done.9 = bf16[512,512]{1,0:T(8,128)(2,1)S(1)} copy-done((bf16[512,512]{1,0:T(8,128)(2,1)S(1)}, bf16[512,512]{1,0:T(8,128)(2,1)}, u32[]{:S(2)}) %copy-start.9) | copy-done | bytes 524312
  18.8 1.0 %copy-done.10 = bf16[512,512]{1,0:T(8,128)(2,1)S(1)} copy-done((bf16[512,512]{1,0:T(8,128)(2,1)S(1)}, bf16[512,512]{1,0:T(8,128)(2,1)}, u32[]{:S(2)}) %copy-start.10) | copy-done | bytes 524312
  19.9 1.0 %copy-done.12 = bf16[512,512]{1,0:T(8,128)(2,1)S(1)} copy-done((bf16[512,512]{1,0:T(8,128)(2,1)S(1)}, bf16[512,512]{1,0:T(8,128)(2,1)}, u32[]{:S(2)}) %copy-start.12) | copy-done | bytes 524312
  20.9 0.9 %copy-done.25 = f32[512,128]{1,0:T(8,128)S(1)} copy-done((f32[512,128]{1,0:T(8,128)S(1)}, f32[512,128]{1,0:T(8,128)}, u32[]{:S(2)}) %copy-start.25) | copy-done | bytes 262168
  21.9 8.8 %attend_chip.1 = (bf16[512,512]{1,0:T(8,128)(2,1)S(1)}, f32[512,512]{1,0:T(8,128)S(1)}, f32[512,512]{1,0:T(8,128)S(1)}, f32[512,128]{1,0:T(8,128)S(1)}) custom-call(s32[1]{0:T(128)} %bitcast.side, bf16[528,512]{1,0:T(8,128)(2,1)S(1)} %get-tuple-element.13.own, bf16[528,512]{1,0:T(8,128)(2,1)S(1)} %copy-done.7, f32[512,128]{1,0:T(8,128)S(1)} %copy-done.25, ...), custom_call_target="tpu_custom_call" | custom-call | flops 5368709120 | bytes 4194304 | tf_op jit(solution)/shard_map/attend_chip/pallas_call | solution.py:292
  30.6 1.0 %copy-done.27 = f32[512,512]{1,0:T(8,128)} copy-done((f32[512,512]{1,0:T(8,128)}, f32[512,512]{1,0:T(8,128)S(1)}, u32[]{:S(2)}) %copy-start.27) | copy-done | bytes 1048600
  31.6 1.0 %copy-done.29 = f32[512,512]{1,0:T(8,128)} copy-done((f32[512,512]{1,0:T(8,128)}, f32[512,512]{1,0:T(8,128)S(1)}, u32[]{:S(2)}) %copy-start.29) | copy-done | bytes 1048600
  32.6 0.8 %copy-done.31 = bf16[512,512]{1,0:T(8,128)(2,1)} copy-done((bf16[512,512]{1,0:T(8,128)(2,1)}, bf16[512,512]{1,0:T(8,128)(2,1)S(1)}, u32[]{:S(2)}) %copy-start.31) | copy-done | bytes 524312
  33.4 0.7 copy-done.33
  34.1 0.0 all-to-all-done
  34.1 0.0 collective-permute-done.other
  34.1 0.0 copy-start.5
  34.2 1.6 %copy-done.5 = bf16[2048,512]{1,0:T(8,128)(2,1)S(1)} copy-done((bf16[2048,512]{1,0:T(8,128)(2,1)S(1)}, bf16[2048,512]{1,0:T(8,128)(2,1)}, u32[]{:S(2)}) %copy-start.5) | copy-done | bytes 2097176
  35.7 1.0 %copy-done.11 = bf16[512,512]{1,0:T(8,128)(2,1)S(1)} copy-done((bf16[512,512]{1,0:T(8,128)(2,1)S(1)}, bf16[512,512]{1,0:T(8,128)(2,1)}, u32[]{:S(2)}) %copy-start.11) | copy-done | bytes 524312
  36.8 1.0 %copy-done.13 = bf16[512,512]{1,0:T(8,128)(2,1)S(1)} copy-done((bf16[512,512]{1,0:T(8,128)(2,1)S(1)}, bf16[512,512]{1,0:T(8,128)(2,1)}, u32[]{:S(2)}) %copy-start.13) | copy-done | bytes 524312
  37.8 1.0 %copy-done.14 = bf16[512,512]{1,0:T(8,128)(2,1)S(1)} copy-done((bf16[512,512]{1,0:T(8,128)(2,1)S(1)}, bf16[512,512]{1,0:T(8,128)(2,1)}, u32[]{:S(2)}) %copy-start.14) | copy-done | bytes 524312
  38.9 1.0 %copy-done.15 = bf16[512,512]{1,0:T(8,128)(2,1)S(1)} copy-done((bf16[512,512]{1,0:T(8,128)(2,1)S(1)}, bf16[512,512]{1,0:T(8,128)(2,1)}, u32[]{:S(2)}) %copy-start.15) | copy-done | bytes 524312
  39.9 0.9 %copy-done.26 = f32[512,128]{1,0:T(8,128)S(1)} copy-done((f32[512,128]{1,0:T(8,128)S(1)}, f32[512,128]{1,0:T(8,128)}, u32[]{:S(2)}) %copy-start.26) | copy-done | bytes 262168
  40.9 1.2 %copy-done.28 = f32[512,512]{1,0:T(8,128)S(1)} copy-done((f32[512,512]{1,0:T(8,128)S(1)}, f32[512,512]{1,0:T(8,128)}, u32[]{:S(2)}) %copy-start.28) | copy-done | bytes 1048600
  42.1 1.2 %copy-done.30 = f32[512,512]{1,0:T(8,128)S(1)} copy-done((f32[512,512]{1,0:T(8,128)S(1)}, f32[512,512]{1,0:T(8,128)}, u32[]{:S(2)}) %copy-start.30) | copy-done | bytes 1048600
  43.3 1.0 %copy-done.32 = bf16[512,512]{1,0:T(8,128)(2,1)S(1)} copy-done((bf16[512,512]{1,0:T(8,128)(2,1)S(1)}, bf16[512,512]{1,0:T(8,128)(2,1)}, u32[]{:S(2)}) %copy-start.32) | copy-done | bytes 524312
  44.4 0.9 %copy-done.34 = f32[512,128]{1,0:T(8,128)S(1)} copy-done((f32[512,128]{1,0:T(8,128)S(1)}, f32[512,128]{1,0:T(8,128)}, u32[]{:S(2)}) %copy-start.34) | copy-done | bytes 262168
  45.3 10.4 %attend_far.1 = (bf16[512,512]{1,0:T(8,128)(2,1)}, bf16[128,512]{1,0:T(8,128)(2,1)S(1)}) custom-call(s32[1]{0:T(128)} %bitcast.side, bf16[528,512]{1,0:T(8,128)(2,1)S(1)} %get-tuple-element.13.own, bf16[528,512]{1,0:T(8,128)(2,1)S(1)} %collective-permute-done.other, f32[512,128]{1,0:T(8,128)S(1)} %copy-done.26, bf16[512,512]{1,0:T(8,128)(2,1)S(1)} %copy-done.32, ...), custom_call_target="tpu_custom_call" | custom-call | flops 5368709120 | bytes 7864320 | tf_op jit(solution)/shard_map/attend_far/pallas_call | solution.py:292
  55.7 0.0 collective-permute-start.2
  55.7 0.0 copy-start.18
  55.7 1.0 %copy-done.18 = bf16[512,512]{1,0:T(8,128)(2,1)S(1)} copy-done((bf16[512,512]{1,0:T(8,128)(2,1)S(1)}, bf16[512,512]{1,0:T(8,128)(2,1)}, u32[]{:S(2)}) %copy-start.18) | copy-done | bytes 524312
  56.8 2.8 %decode_own.1 = (f32[128,512]{1,0:T(8,128)S(1)}, f32[128,512]{1,0:T(8,128)S(1)}, f32[128,128]{1,0:T(8,128)S(1)}) custom-call(bf16[512,512]{1,0:T(8,128)(2,1)S(1)} %copy-done.18, bf16[128,512]{1,0:T(8,128)(2,1)S(1)} %get-tuple-element.20.dq, bf16[512,512]{1,0:T(8,128)(2,1)S(1)} %copy-done.16, bf16[512,512]{1,0:T(8,128)(2,1)S(1)} %copy-done.17), custom_call_target="tpu_custom_call" | custom-call | flops 1073741824 | bytes 2097152 | tf_op jit(solution)/shard_map/decode_own/pallas_call | solution.py:292
  59.6 0.0 collective-permute-done.2.enc
  59.6 0.0 copy-start
  59.6 0.0 copy-start.1
  59.6 0.0 copy-start.2
  59.7 0.0 copy-start.3
  59.7 3.2 %decode_other.1 = bf16[128,640]{1,0:T(8,128)(2,1)S(1)} custom-call(bf16[512,512]{1,0:T(8,128)(2,1)S(1)} %collective-permute-done.2.enc, bf16[128,512]{1,0:T(8,128)(2,1)S(1)} %get-tuple-element.20.dq, f32[128,512]{1,0:T(8,128)S(1)} %get-tuple-element.21.out1, f32[128,512]{1,0:T(8,128)S(1)} %get-tuple-element.22.total1, ...), custom_call_target="tpu_custom_call" | custom-call | flops 1073741824 | bytes 2097152 | tf_op jit(solution)/shard_map/decode_other/pallas_call | solution.py:292
  62.9 13.8 %all_to_all.10.parts = bf16[8,16,640]{2,1,0:T(8,128)(2,1)S(1)} all-to-all(bf16[8,16,640]{2,1,0:T(8,128)(2,1)S(1)} %bitcast.8), channel_id=1, replica_groups=mesh['groups'=2,'hit'=8,'query'=2] {'hit'}, dimensions={0} | all-to-all | bytes 327680 | tf_op jit(solution)/shard_map/all_to_all | solution.py:398
  76.7 1.4 %merge_spans.1 = bf16[16,512]{1,0:T(8,128)(2,1)} custom-call(bf16[8,16,640]{2,1,0:T(8,128)(2,1)S(1)} %all_to_all.10.parts, bf16[16,512]{1,0:T(8,128)(2,1)S(1)} %copy-done.2, bf16[512,512]{1,0:T(8,128)(2,1)S(1)} %copy-done, f32[1,512]{1,0:T(1,128)S(1)} %bitcast.10, bf16[512,512]{1,0:T(8,128)(2,1)S(1)} %copy-done.1), custom_call_target="tpu_custom_call" | custom-call | flops 16777216 | bytes 1048576 | tf_op jit(solution)/shard_map/merge_spans/pallas_call | solution.py:292
  (38 shorter events, 0.1 us)
Async XLA Ops:
  0.6 1.0 %copy-start.8 = (bf16[512,512]{1,0:T(8,128)(2,1)S(1)}, bf16[512,512]{1,0:T(8,128)(2,1)}, u32[]{:S(2)}) copy-start(bf16[512,512]{1,0:T(8,128)(2,1)} %hits.1) | copy-start | bytes 1572868
  1.7 0.7 copy-start.19
  2.4 0.7 copy-start.20
  3.0 0.7 copy-start.21
  4.3 0.7 copy-start.24
  5.0 10.9 %collective-permute-start.1 = (bf16[528,512]{1,0:T(8,128)(2,1)S(1)}, bf16[528,512]{1,0:T(8,128)(2,1)S(1)}, u32[]{:S(2)}, u32[]{:S(2)}) collective-permute-start(bf16[528,512]{1,0:T(8,128)(2,1)S(1)} %get-tuple-element.13.own), channel_id=1, source_target_pairs={{0,1},{1,0},{2,3},{3,2},{4,5},{5,4},{6,7},{7,6},{8,9},{9,8},{10,11... | collective-permute-start | bytes 1622024 | tf_op jit(solution)/shard_map/ppermute | solution.py:337
  5.5 28.6 %collective-permute-start = (bf16[528,512]{1,0:T(8,128)(2,1)S(1)}, bf16[528,512]{1,0:T(8,128)(2,1)S(1)}, u32[]{:S(2)}, u32[]{:S(2)}) collective-permute-start(bf16[528,512]{1,0:T(8,128)(2,1)S(1)} %get-tuple-element.13.own), channel_id=1, source_target_pairs={{0,15},{1,2},{2,1},{3,4},{4,3},{5,6},{6,5},{7,8},{8,7},{9,10},{10,... | collective-permute-start | bytes 1622024 | tf_op jit(solution)/shard_map/ppermute | solution.py:336
  12.5 21.6 %all-to-all-start = ((bf16[8,16,512]{2,1,0:T(8,128)(2,1)}), bf16[8,16,512]{2,1,0:T(8,128)(2,1)S(1)}, u32[]{:S(2)}, u32[]{:S(2)}) async-start(bf16[8,16,512]{2,1,0:T(8,128)(2,1)} %broadcast_in_dim.25), calls=%async_computation | async-start | bytes 262144 | tf_op jit(solution)/shard_map/all_to_all | solution.py:323
  15.9 0.8 %copy-start.6 = (bf16[528,512]{1,0:T(8,128)(2,1)}, bf16[528,512]{1,0:T(8,128)(2,1)S(1)}, u32[]{:S(2)}) copy-start(bf16[528,512]{1,0:T(8,128)(2,1)S(1)} %collective-permute-done.1.other) | copy-start | bytes 1622020
  16.7 1.0 %copy-start.7 = (bf16[528,512]{1,0:T(8,128)(2,1)S(1)}, bf16[528,512]{1,0:T(8,128)(2,1)}, u32[]{:S(2)}) copy-start(bf16[528,512]{1,0:T(8,128)(2,1)} %copy-done.6) | copy-start | bytes 1622020
  17.8 1.0 %copy-start.9 = (bf16[512,512]{1,0:T(8,128)(2,1)S(1)}, bf16[512,512]{1,0:T(8,128)(2,1)}, u32[]{:S(2)}) copy-start(bf16[512,512]{1,0:T(8,128)(2,1)} %wq.1) | copy-start | bytes 1572868
  18.8 1.0 %copy-start.10 = (bf16[512,512]{1,0:T(8,128)(2,1)S(1)}, bf16[512,512]{1,0:T(8,128)(2,1)}, u32[]{:S(2)}) copy-start(bf16[512,512]{1,0:T(8,128)(2,1)} %wk.5) | copy-start | bytes 1572868
  19.9 1.0 %copy-start.12 = (bf16[512,512]{1,0:T(8,128)(2,1)S(1)}, bf16[512,512]{1,0:T(8,128)(2,1)}, u32[]{:S(2)}) copy-start(bf16[512,512]{1,0:T(8,128)(2,1)} %wv.5) | copy-start | bytes 1572868
  20.9 0.9 %copy-start.25 = (f32[512,128]{1,0:T(8,128)S(1)}, f32[512,128]{1,0:T(8,128)}, u32[]{:S(2)}) copy-start(f32[512,128]{1,0:T(8,128)} %copy-done.24) | copy-start | bytes 786436
  21.9 12.3 %copy-start.4 = (bf16[512,2048]{1,0:T(8,128)(2,1)S(1)}, bf16[512,2048]{1,0:T(8,128)(2,1)}, u32[]{:S(2)}) copy-start(bf16[512,2048]{1,0:T(8,128)(2,1)} %up.1) | copy-start | bytes 6291460
  21.9 12.3 %copy-start.22 = (f32[512]{0:T(512)S(1)}, f32[512]{0:T(512)}, u32[]{:S(2)}) copy-start(f32[512]{0:T(512)} %param.27) | copy-start | bytes 6148
  21.9 12.3 %copy-start.23 = (f32[512]{0:T(512)S(1)}, f32[512]{0:T(512)}, u32[]{:S(2)}) copy-start(f32[512]{0:T(512)} %param.30) | copy-start | bytes 6148
  30.6 1.0 %copy-start.27 = (f32[512,512]{1,0:T(8,128)}, f32[512,512]{1,0:T(8,128)S(1)}, u32[]{:S(2)}) copy-start(f32[512,512]{1,0:T(8,128)S(1)} %get-tuple-element.16.out1) | copy-start | bytes 3145732
  31.6 1.0 %copy-start.29 = (f32[512,512]{1,0:T(8,128)}, f32[512,512]{1,0:T(8,128)S(1)}, u32[]{:S(2)}) copy-start(f32[512,512]{1,0:T(8,128)S(1)} %get-tuple-element.17.total1) | copy-start | bytes 3145732
  32.6 0.8 %copy-start.31 = (bf16[512,512]{1,0:T(8,128)(2,1)}, bf16[512,512]{1,0:T(8,128)(2,1)S(1)}, u32[]{:S(2)}) copy-start(bf16[512,512]{1,0:T(8,128)(2,1)S(1)} %get-tuple-element.15.query) | copy-start | bytes 1572868
  33.4 0.7 copy-start.33
  34.1 1.6 %copy-start.5 = (bf16[2048,512]{1,0:T(8,128)(2,1)S(1)}, bf16[2048,512]{1,0:T(8,128)(2,1)}, u32[]{:S(2)}) copy-start(bf16[2048,512]{1,0:T(8,128)(2,1)} %down.1) | copy-start | bytes 6291460
  35.7 1.0 %copy-start.11 = (bf16[512,512]{1,0:T(8,128)(2,1)S(1)}, bf16[512,512]{1,0:T(8,128)(2,1)}, u32[]{:S(2)}) copy-start(bf16[512,512]{1,0:T(8,128)(2,1)} %wk.5) | copy-start | bytes 1572868
  36.8 1.0 %copy-start.13 = (bf16[512,512]{1,0:T(8,128)(2,1)S(1)}, bf16[512,512]{1,0:T(8,128)(2,1)}, u32[]{:S(2)}) copy-start(bf16[512,512]{1,0:T(8,128)(2,1)} %wv.5) | copy-start | bytes 1572868
  37.8 1.0 %copy-start.14 = (bf16[512,512]{1,0:T(8,128)(2,1)S(1)}, bf16[512,512]{1,0:T(8,128)(2,1)}, u32[]{:S(2)}) copy-start(bf16[512,512]{1,0:T(8,128)(2,1)} %wo.2) | copy-start | bytes 1572868
  38.9 1.0 %copy-start.15 = (bf16[512,512]{1,0:T(8,128)(2,1)S(1)}, bf16[512,512]{1,0:T(8,128)(2,1)}, u32[]{:S(2)}) copy-start(bf16[512,512]{1,0:T(8,128)(2,1)} %dec_wq.1) | copy-start | bytes 1572868
  39.9 0.9 %copy-start.26 = (f32[512,128]{1,0:T(8,128)S(1)}, f32[512,128]{1,0:T(8,128)}, u32[]{:S(2)}) copy-start(f32[512,128]{1,0:T(8,128)} %copy-done.24) | copy-start | bytes 786436
  40.9 1.2 %copy-start.28 = (f32[512,512]{1,0:T(8,128)S(1)}, f32[512,512]{1,0:T(8,128)}, u32[]{:S(2)}) copy-start(f32[512,512]{1,0:T(8,128)} %copy-done.27) | copy-start | bytes 3145732
  42.1 1.2 %copy-start.30 = (f32[512,512]{1,0:T(8,128)S(1)}, f32[512,512]{1,0:T(8,128)}, u32[]{:S(2)}) copy-start(f32[512,512]{1,0:T(8,128)} %copy-done.29) | copy-start | bytes 3145732
  43.3 1.0 %copy-start.32 = (bf16[512,512]{1,0:T(8,128)(2,1)S(1)}, bf16[512,512]{1,0:T(8,128)(2,1)}, u32[]{:S(2)}) copy-start(bf16[512,512]{1,0:T(8,128)(2,1)} %copy-done.31) | copy-start | bytes 1572868
  44.4 0.9 %copy-start.34 = (f32[512,128]{1,0:T(8,128)S(1)}, f32[512,128]{1,0:T(8,128)}, u32[]{:S(2)}) copy-start(f32[512,128]{1,0:T(8,128)} %copy-done.33) | copy-start | bytes 786436
  45.3 10.4 %copy-start.16 = (bf16[512,512]{1,0:T(8,128)(2,1)S(1)}, bf16[512,512]{1,0:T(8,128)(2,1)}, u32[]{:S(2)}) copy-start(bf16[512,512]{1,0:T(8,128)(2,1)} %wk.7) | copy-start | bytes 1572868
  45.3 10.4 %copy-start.17 = (bf16[512,512]{1,0:T(8,128)(2,1)S(1)}, bf16[512,512]{1,0:T(8,128)(2,1)}, u32[]{:S(2)}) copy-start(bf16[512,512]{1,0:T(8,128)(2,1)} %wv.7) | copy-start | bytes 1572868
  55.7 3.9 %collective-permute-start.2 = (bf16[512,512]{1,0:T(8,128)(2,1)}, bf16[512,512]{1,0:T(8,128)(2,1)S(1)}, u32[]{:S(2)}, u32[]{:S(2)}) collective-permute-start(bf16[512,512]{1,0:T(8,128)(2,1)} %get-tuple-element.11.enc), channel_id=1, source_target_pairs={{0,1},{1,0},{2,3},{3,2},{4,5},{5,4},{6,7},{7,6},{8,9},{9,8},{10,11... | collective-permute-start | bytes 1572872 | tf_op jit(solution)/shard_map/ppermute | solution.py:375
  55.7 1.0 %copy-start.18 = (bf16[512,512]{1,0:T(8,128)(2,1)S(1)}, bf16[512,512]{1,0:T(8,128)(2,1)}, u32[]{:S(2)}) copy-start(bf16[512,512]{1,0:T(8,128)(2,1)} %get-tuple-element.11.enc) | copy-start | bytes 1572868
  59.6 17.1 %copy-start = (bf16[512,512]{1,0:T(8,128)(2,1)S(1)}, bf16[512,512]{1,0:T(8,128)(2,1)}, u32[]{:S(2)}) copy-start(bf16[512,512]{1,0:T(8,128)(2,1)} %wo.3) | copy-start | bytes 1572868
  59.6 17.1 %copy-start.1 = (bf16[512,512]{1,0:T(8,128)(2,1)S(1)}, bf16[512,512]{1,0:T(8,128)(2,1)}, u32[]{:S(2)}) copy-start(bf16[512,512]{1,0:T(8,128)(2,1)} %proj.1) | copy-start | bytes 1572868
  59.6 17.1 %copy-start.2 = (bf16[16,512]{1,0:T(8,128)(2,1)S(1)}, bf16[16,512]{1,0:T(8,128)(2,1)}, u32[]{:S(2)}) copy-start(bf16[16,512]{1,0:T(8,128)(2,1)} %objects.1) | copy-start | bytes 49156
  59.7 17.1 %copy-start.3 = (f32[512]{0:T(512)S(1)}, f32[512]{0:T(512)}, u32[]{:S(2)}) copy-start(f32[512]{0:T(512)} %param.36) | copy-start | bytes 6148
